TPU v7x, 32 devices: a whole 2x2x4 slice. The times are simulated.
32 devices in a mesh: ch: 4 (over y, x), row: 8 (over z, core).
Axes of the slice: x: 2, y: 2, z: 4, core: 2. Of those that a mesh axis runs over, the one named last changes fastest.
Arguments:
- latent: bfloat16 [128, 32, 1280], P('row', None, 'ch'), may hold values from -50 to 50
- timestep: int32 [4], replicated, may hold values from 0 to 999
- norm_gain_a: float32 [1280], P('ch'), may hold values from 0.1 to 1.9
- conv_weight_a: bfloat16 [1280, 3, 3, 1280], P('ch'), may hold values from -0.0546875 to 0.0546875
- time_weight: bfloat16 [320, 1280], P(None, 'ch'), may hold values from -0.3125 to 0.3125
- norm_gain_b: float32 [1280], P('ch'), may hold values from 0.1 to 1.9
- conv_weight_b: bfloat16 [1280, 3, 3, 1280], P('ch'), may hold values from -0.0546875 to 0.0546875
- norm_gain_c: float32 [1280], P('ch'), may hold values from 0.1 to 1.9
- w_query: bfloat16 [1024, 1280], P('ch'), may hold values from -4 to 4
- w_key: bfloat16 [1024, 1280], P('ch'), may hold values from -4 to 4
- w_value: bfloat16 [1024, 1280], P('ch'), may hold values from -0.3125 to 0.3125
- w_out: bfloat16 [1280, 1024], P('ch'), may hold values from -0.1875 to 0.1875
Outputs:
- result: bfloat16 [128, 32, 1280], P('row', None, 'ch')
All inputs are finite; a program needn't handle non-finite values.
Results may differ from a plain program's by a relative error of at most 0.017.
Values may be sent and summed in bfloat16 or wider, within the bound.
A program may use at most 64 MiB of HBM per device.

v0:
```python
import math

import jax
import jax.numpy as jnp
from jax import lax
from jax.sharding import PartitionSpec as P

C = 1280
GROUPS = 32
HEAD_DIM = 64
TDIM = 320
H = 32


eps_value = 1e-06


def swapped(value, axis, stride):
    mask = 2**stride
    pairs = [(source, source ^ mask) for source in range(lax.axis_size(axis))]
    return lax.ppermute(value, axis, pairs)


def right_product(left, weight):
    return lax.dot_general(
        left, weight, (((1,), (1,)), ((), ())), preferred_element_type=jnp.float32
    )


def conv_taps(padded, weight):
    outcome = lax.conv_general_dilated(
        padded[None],
        weight,
        (1, 1),
        "VALID",
        dimension_numbers=("NHWC", "OHWI", "NHWC"),
        preferred_element_type=jnp.float32,
    )
    return outcome[0]


def pad_columns(field):
    return jnp.pad(field, ((0, 0), (1, 1), (0, 0)))


def body(
    latent,
    timestep,
    norm_gain_a,
    conv_weight_a,
    time_weight,
    norm_gain_b,
    conv_weight_b,
    norm_gain_c,
    w_query,
    w_key,
    w_value,
    w_out,
):
    rows, width, local_ch = latent.shape
    span = H // rows
    place = lax.axis_index("row")
    within = place % span
    image_id = place // span
    group_width = C // GROUPS
    local_groups = local_ch // group_width
    members = float(H * width * group_width)
    tokens = rows * width

    def group_norm(value, gain):
        flat = value.reshape(tokens, local_groups, group_width)
        stats = jnp.stack([jnp.sum(flat, axis=(0, 2)), jnp.sum(flat * flat, axis=(0, 2))])
        stats = stats + swapped(stats, "row", 0)
        mean = stats[0] / members
        spread = stats[1] / members - mean * mean
        scaled = (flat - mean[None, :, None]) * lax.rsqrt(spread + eps_value)[None, :, None]
        return scaled.reshape(rows, width, local_ch) * gain

    upper_half = within == 0

    def facing_row(field):
        return jnp.where(upper_half, field[-1:], field[:1])

    def attach_rim(field, partner):
        empty_row = jnp.zeros_like(partner)
        above = jnp.where(upper_half, empty_row, partner)
        below = jnp.where(upper_half, partner, empty_row)
        return jnp.concatenate([above, field, below], axis=0)

    def convolve(active, weight):
        full = lax.all_gather(active, "ch", axis=2, tiled=True)
        partner = swapped(facing_row(full), "row", 0)
        rimmed = attach_rim(full, partner)
        result_conv = conv_taps(pad_columns(rimmed), weight)
        return result_conv

    image_ids = jnp.arange(timestep.shape[0])
    step_value = jnp.sum(jnp.where(image_ids == image_id, timestep, 0)).astype(jnp.float32)
    half = TDIM // 2
    freqs = jnp.exp(-math.log(10000.0) * jnp.arange(half, dtype=jnp.float32) / half)
    angles = step_value * freqs
    sinus = jnp.concatenate([jnp.cos(angles), jnp.sin(angles)])[None, :].astype(jnp.bfloat16)
    time_add = jax.nn.silu(jnp.dot(sinus, time_weight, preferred_element_type=jnp.float32))
    source = latent.astype(jnp.float32)
    active_a = jax.nn.silu(group_norm(source, norm_gain_a)).astype(jnp.bfloat16)
    hidden_a = convolve(active_a, conv_weight_a) + time_add[None]
    active_b = jax.nn.silu(group_norm(hidden_a, norm_gain_b)).astype(jnp.bfloat16)
    hidden_b = source + convolve(active_b, conv_weight_b)
    normed = group_norm(hidden_b, norm_gain_c).astype(jnp.bfloat16).reshape(tokens, local_ch)
    inner = w_query.shape[0]
    projections = jnp.concatenate([w_query, w_key, w_value], axis=0)
    weight_cols = projections
    mixed = right_product(lax.all_gather(normed, "ch", axis=1, tiled=True), weight_cols)
    query = mixed[:, :inner].astype(jnp.bfloat16)
    keyed = mixed[:, inner : 2 * inner].astype(jnp.bfloat16)
    valued = mixed[:, 2 * inner :].astype(jnp.bfloat16)
    key_value = jnp.stack([keyed, valued])
    key_value = jnp.concatenate([key_value, swapped(key_value, "row", 0)], axis=1)
    local_heads = inner // HEAD_DIM
    query_heads = query.reshape(tokens, local_heads, HEAD_DIM)
    key_heads = key_value[0].reshape(-1, local_heads, HEAD_DIM)
    value_heads = key_value[1].reshape(-1, local_heads, HEAD_DIM)
    scores = jnp.einsum(
        "qhd,khd->hqk", query_heads, key_heads, preferred_element_type=jnp.float32
    ) * (1.0 / math.sqrt(HEAD_DIM))
    highest = jnp.max(scores, axis=-1, keepdims=True)
    raised = jnp.exp(scores - highest)
    weights = (raised / jnp.sum(raised, axis=-1, keepdims=True)).astype(jnp.bfloat16)
    heads_out = jnp.einsum("hqk,khd->qhd", weights, value_heads, preferred_element_type=jnp.float32)
    heads_out = heads_out.astype(jnp.bfloat16).reshape(tokens, inner)
    weight_cols = w_out
    projected = right_product(lax.all_gather(heads_out, "ch", axis=1, tiled=True), weight_cols)
    total = hidden_b.reshape(tokens, local_ch) + projected
    return total.reshape(rows, width, local_ch).astype(jnp.bfloat16)


def solution(mesh):
    return jax.shard_map(
        body,
        mesh=mesh,
        in_specs=(
            P("row", None, "ch"),
            P(),
            P("ch"),
            P("ch", None, None, None),
            P(None, "ch"),
            P("ch"),
            P("ch", None, None, None),
            P("ch"),
            P("ch", None),
            P("ch", None),
            P("ch", None),
            P("ch", None),
        ),
        out_specs=P("row", None, "ch"),
        check_vma=False,
    )
```

profile of v0, /device:TPU:0, one launch (start us, length us, event | category | flops | bytes accessed | tf_op | source)
XLA Modules:
  0.0 277.8 jit_solution(7291214916432832792)
XLA Ops:
  6.5 1.3 convert_reduce_fusion
  9.9 1.3 fusion.55
  11.2 1.8 copy.96
  14.7 62.4 %all-gather.5.cloned.1.call-done = bf16[16,32,1280]{1,0,2:T(8,128)(2,1)} async-done(((bf16[16,32,320]{1,0,2:T(8,128)(2,1)}), bf16[16,32,1280]{1,0,2:T(8,128)(2,1)}) %all-gather.5.cloned.1.call-update) | async-done | bytes 1310736 | tf_op jit(solution)/shard_map/all_gather | solution.py:91
  77.1 3.0 %broadcast_select_fusion.5 = bf16[1,32,1280]{1,0,2:T(2,128)(2,1)S(1)} fusion(pred[]{:T(512)S(6)} %eq.11, bf16[16,32,1280]{1,0,2:T(8,128)(2,1)} %all-gather.5.cloned.1.call-done), kind=kLoop, calls=%fused_computation.48 | loop fusion | flops 40960 | bytes 245761 | tf_op jit(solution)/shard_map/jit(_where)/select_n | solution.py:82
  80.6 6.0 %copy.101 = bf16[16,32,1280]{2,1,0:T(8,128)(2,1)S(1)} copy(bf16[16,32,1280]{1,0,2:T(8,128)(2,1)} %all-gather.5.cloned.1.call-done) | data formatting | bytes 2621440 | tf_op jit(solution)/shard_map/all_gather | solution.py:91
  87.1 1.9 broadcast_select_fusion.4
  89.0 1.3 copy.100
  92.3 1.1 slice-done
  94.5 7.8 %select_reduce_fusion.1 = (f32[320]{0:T(512)S(1)}, f32[320]{0:T(512)S(1)}, f32[16,8,5,320]{3,1,2,0:T(8,128)S(1)}) fusion(f32[320]{0:T(512)S(1)} %divide_multiply_fusion, pred[8,5]{0,1:T(8,128)(4,1)S(1)} %copy-done.8, bf16[320,3,3,1280]{3,0,2,1:T(8,128)(2,1)S(1)} %bitcast.121, bf16[18,1,7,2,1280]{4,2,3,0,1:T(8,128)(2,1)S(1)} %slice.69, ...), kind=kOutput, calls=%fused_computation.59 | convolution fusion | flops 4727766016 | bytes 10684200 | tf_op jit(solution)/shard_map/conv_general_dilated | solution.py:31
  104.8 2.0 copy.107
  106.8 61.4 %all-gather.7.cloned.1.call-done = bf16[16,32,1280]{1,0,2:T(8,128)(2,1)} async-done(((bf16[16,32,320]{1,0,2:T(8,128)(2,1)}), bf16[16,32,1280]{1,0,2:T(8,128)(2,1)}) %all-gather.7.cloned.1.call-update) | async-done | bytes 1310736 | tf_op jit(solution)/shard_map/all_gather | solution.py:91
  168.2 3.0 %broadcast_select_fusion.2 = bf16[1,32,1280]{1,0,2:T(2,128)(2,1)S(1)} fusion(pred[]{:T(512)S(6)} %eq.11, bf16[16,32,1280]{1,0,2:T(8,128)(2,1)} %all-gather.7.cloned.1.call-done), kind=kLoop, calls=%fused_computation.45 | loop fusion | flops 40960 | bytes 245761 | tf_op jit(solution)/shard_map/jit(_where)/select_n | solution.py:82
  171.7 6.0 %copy.112 = bf16[16,32,1280]{2,1,0:T(8,128)(2,1)S(1)} copy(bf16[16,32,1280]{1,0,2:T(8,128)(2,1)} %all-gather.7.cloned.1.call-done) | data formatting | bytes 2621440 | tf_op jit(solution)/shard_map/all_gather | solution.py:91
  178.2 1.9 broadcast_select_fusion.1
  180.1 1.3 copy.111
  185.6 7.8 %fusion.35 = f32[16,8,5,320]{3,1,2,0:T(8,128)S(1)} fusion(bf16[320,3,3,1280]{3,0,2,1:T(8,128)(2,1)S(1)} %bitcast.123, bf16[18,1,7,2,1280]{4,2,3,0,1:T(8,128)(2,1)S(1)} %slice.73, bf16[18,1,8,5,1280]{4,2,3,0,1:T(8,128)(2,1)S(1)} %copy.116, pred[8,5]{0,1:T(8,128)(4,1)S(1)} %copy-done.8), kind=kOutput, calls=%fused_computation.49 | convolution fusion | flops 4726538240 | bytes 10680360 | tf_op jit(solution)/shard_map/conv_general_dilated | solution.py:31
  197.2 28.8 %all-gather.9.cloned.1.call-done = bf16[512,1280]{0,1:T(8,128)(2,1)} async-done(((bf16[512,320]{0,1:T(8,128)(2,1)}), bf16[512,1280]{0,1:T(8,128)(2,1)}) %all-gather.9.cloned.1.call-update) | async-done | bytes 1310736 | tf_op jit(solution)/shard_map/all_gather | solution.py:113
  225.9 2.7 fusion.32
  229.0 1.7 collective-permute-done.5
  231.3 5.0 %fusion.81 = (f32[4,512]{1,0:T(4,128)S(1)}, f32[4,512,1024]{2,1,0:T(8,128)}) fusion(bf16[512,4,64]{0,2,1:T(8,128)(2,1)S(1)} %bitcast.106, bf16[1024,4,64]{0,2,1:T(8,128)(2,1)S(1)} %bitcast.104), kind=kOutput, calls=%fused_computation.118 | convolution fusion | flops 274727936 | bytes 9183232 | tf_op jit(solution)/shard_map/sub | solution.py:127
  236.4 5.5 %fusion.44 = bf16[4,64,512]{2,1,0:T(8,128)(2,1)} fusion(bf16[1024,4,64]{0,2,1:T(8,128)(2,1)S(1)} %bitcast.105, f32[4,512,1024]{2,1,0:T(8,128)} %get-tuple-element.23, f32[4,512]{1,0:T(4,128)S(1)} %get-tuple-element.22), kind=kOutput, calls=%fused_computation.55 | convolution fusion | flops 272760832 | bytes 9183232 | tf_op jit(solution)/shard_map/hqk,khd->qhd/dot_general | solution.py:129
  242.5 26.1 %all-gather.11.cloned.1.call-done = bf16[512,1024]{0,1:T(8,128)(2,1)} async-done(((bf16[512,256]{0,1:T(8,128)(2,1)}), bf16[512,1024]{0,1:T(8,128)(2,1)}) %all-gather.11.cloned.1.call-update) | async-done | bytes 1048592 | tf_op jit(solution)/shard_map/all_gather | solution.py:132
  268.6 1.7 fusion.43
  (121 shorter events, 20.7 us)
Async XLA Ops:
  6.5 262.1 %copy-start = (bf16[320,1024]{1,0:T(8,128)(2,1)S(1)}, bf16[320,1024]{1,0:T(8,128)(2,1)}, u32[]{:S(2)}) copy-start(bf16[320,1024]{1,0:T(8,128)(2,1)} %param.23) | copy-start | bytes 1966084
  6.5 6.6 %copy-start.7 = (s32[4]{0:T(128)S(1)}, s32[4]{0:T(128)}, u32[]{:S(2)}) copy-start(s32[4]{0:T(128)} %param.13) | copy-start | bytes 52
  6.5 8.0 %copy-start.2 = (bf16[320,320]{1,0:T(8,128)(2,1)S(1)}, bf16[320,320]{1,0:T(8,128)(2,1)}, u32[]{:S(2)}) copy-start(bf16[320,320]{1,0:T(8,128)(2,1)} %param.16) | copy-start | bytes 614404
  6.5 70.5 %all-gather.5.cloned.1.call-start = ((), (), s32[]{:S(2)}) async-start(), calls=%async_computation | async-start | bytes 6553600 | tf_op jit(solution)/shard_map/all_gather | solution.py:91
  8.2 1.4 collective-permute-start
  13.0 155.2 %all-gather.7.cloned.1.call-start = ((), (), s32[]{:S(2)}) async-start(), calls=%async_computation.1 | async-start | bytes 6553600 | tf_op jit(solution)/shard_map/all_gather | solution.py:91
  80.5 6.1 %collective-permute-start.1 = (bf16[1,32,1280]{2,1,0:T(8,128)(2,1)S(1)}, bf16[1,32,1280]{2,1,0:T(8,128)(2,1)S(1)}, u32[]{:S(2)}, u32[]{:S(2)}) collective-permute-start(bf16[1,32,1280]{2,1,0:T(8,128)(2,1)S(1)} %copy.97), channel_id=1, source_target_pairs={{0,1},{1,0},{2,3},{3,2},{4,5},{5,4},{6,7},{7,6},{8,9},{9,8},{10,11... | collective-permute-start | bytes 245768 | tf_op jit(solution)/shard_map/ppermute | solution.py:21
  91.3 2.2 slice-start
  91.6 2.9 %slice-start.1 = ((s8[7372800]{0:T(1024)(128)(4,1)}), s8[3178496]{0:T(1024)(128)(4,1)S(1)}, s32[]{:S(2)}) async-start(s8[7372800]{0:T(1024)(128)(4,1)} %bitcast.120), calls=%async_computation.5 | async-start | bytes 6356992
  91.8 2.7 copy-start.8
  94.5 10.0 %copy-start.3 = (f32[320]{0:T(512)S(1)}, f32[320]{0:T(512)}, u32[]{:S(2)}) copy-start(f32[320]{0:T(512)} %param.17) | copy-start | bytes 3844
  102.8 1.4 collective-permute-start.2
  106.8 119.2 %all-gather.9.cloned.1.call-start = ((), (), s32[]{:S(2)}) async-start(), calls=%async_computation.2 | async-start | bytes 1638400 | tf_op jit(solution)/shard_map/all_gather | solution.py:113
  171.6 6.1 %collective-permute-start.3 = (bf16[1,32,1280]{2,1,0:T(8,128)(2,1)S(1)}, bf16[1,32,1280]{2,1,0:T(8,128)(2,1)S(1)}, u32[]{:S(2)}, u32[]{:S(2)}) collective-permute-start(bf16[1,32,1280]{2,1,0:T(8,128)(2,1)S(1)} %copy.108), channel_id=1, source_target_pairs={{0,1},{1,0},{2,3},{3,2},{4,5},{5,4},{6,7},{7,6},{8,9},{9,8},{10,11... | collective-permute-start | bytes 245768 | tf_op jit(solution)/shard_map/ppermute | solution.py:21
  182.4 2.2 slice-start.2
  182.7 2.9 %slice-start.3 = ((s8[7372800]{0:T(1024)(128)(4,1)}), s8[3178496]{0:T(1024)(128)(4,1)S(1)}, s32[]{:S(2)}) async-start(s8[7372800]{0:T(1024)(128)(4,1)} %bitcast.122), calls=%async_computation.7 | async-start | bytes 6356992
  185.6 8.0 %copy-start.1 = (bf16[16,32,320]{2,1,0:T(8,128)(2,1)S(1)}, bf16[16,32,320]{2,1,0:T(8,128)(2,1)}, u32[]{:S(2)}) copy-start(bf16[16,32,320]{2,1,0:T(8,128)(2,1)} %param.12) | copy-start | bytes 983044
  193.4 2.6 copy-start.4
  193.6 32.3 %copy-start.5 = (bf16[256,1280]{1,0:T(8,128)(2,1)S(1)}, bf16[256,1280]{1,0:T(8,128)(2,1)}, u32[]{:S(2)}) copy-start(bf16[256,1280]{1,0:T(8,128)(2,1)} %param.22) | copy-start | bytes 1966084
  193.6 32.3 %copy-start.6 = (bf16[256,1280]{1,0:T(8,128)(2,1)S(1)}, bf16[256,1280]{1,0:T(8,128)(2,1)}, u32[]{:S(2)}) copy-start(bf16[256,1280]{1,0:T(8,128)(2,1)} %param.21) | copy-start | bytes 1966084
  194.3 1.4 collective-permute-start.4
  197.1 71.5 %all-gather.11.cloned.1.call-start = ((), (), s32[]{:S(2)}) async-start(), calls=%async_computation.3 | async-start | bytes 1310720 | tf_op jit(solution)/shard_map/all_gather | solution.py:132
  228.8 2.0 collective-permute-start.5
Sparse Core Ops, SparseCore 0:
  13.2 63.8 all-gather.4
  106.9 61.2 all-gather.6
  197.2 28.6 all-gather.8
  242.1 26.4 all-gather.10
where the time goes:
time: 278 us
  waiting for transfers between devices  183 us (66%)
  local copies, waits for them, and re-layouts  32 us (12%)
  matrix products  30.8 us (11%)
  other arithmetic  15.9 us (6%)
  between operations  14.3 us (5%)
    all_gather x2, waiting for transfers between devices, convolve(): full = lax.all_gather(active, 'ch', axis=2, tiled=True)  124 us
    all_gather x1, waiting for transfers between devices, body(): lax.all_gather(normed, 'ch', axis=1, tiled=True)  28.8 us
    all_gather x1, waiting for transfers between devices, body(): lax.all_gather(heads_out, 'ch', axis=1, tiled=True)  26.1 us
    conv_general_dilated x2, matrix products, conv_taps(): lax.conv_general_dilated(padded[None], weight, (1, 1), 'VALID', dimension...  15.6 us
    all_gather x2, local copies, waits for them, and re-layouts, convolve(): full = lax.all_gather(active, 'ch', axis=2, tiled=True)  12 us
    select_n x2, other arithmetic, facing_row(): return jnp.where(upper_half, field[-1:], field[:1])  6.06 us
  transfers between devices with their start and end apart: 10, of which 8 were waited for; matrix products, arithmetic and copies ran while one was open for 5% of the time, Pallas kernels for 0%

commit v1 on v0

v1 whole, which is shorter than its diff:
```python
import functools
import math

import jax
import jax.numpy as jnp
from jax import lax
from jax.experimental import pallas as pl
from jax.experimental.pallas import tpu as pltpu
from jax.sharding import PartitionSpec as P

C = 1280
GROUPS = 32
HEAD_DIM = 64
TDIM = 320
H = 32


eps_value = 1e-06
MESH = pl.DeviceIdType.MESH


def swapped(value, axis, stride):
    mask = 2**stride
    pairs = [(source, source ^ mask) for source in range(lax.axis_size(axis))]
    return lax.ppermute(value, axis, pairs)


def right_product(left, weight):
    return lax.dot_general(
        left, weight, (((1,), (1,)), ((), ())), preferred_element_type=jnp.float32
    )


def flipped(place, bit):
    return place + bit * (1 - 2 * ((place // bit) % 2))


def combined(place, other, steps):
    total = 0
    for step in range(steps):
        bit = 2**step
        total = total + bit * (((place // bit) + (other // bit)) % 2)
    return total


def norm_kernel(active, block, group_width, members, *refs):
    value_ref, near, far, gain = refs[:4]
    outs = refs[4:]
    tokens, chunk = value_ref.shape
    main = outs[0].shape[1]

    lane_group = lax.broadcasted_iota(jnp.int32, (chunk, chunk), 1) // group_width
    depth_group = lax.broadcasted_iota(jnp.int32, (chunk, chunk), 0) // group_width
    same = jnp.where(lane_group == depth_group, 1.0, 0.0)
    stats = jnp.dot(
        near[...] + far[...], same, precision=lax.Precision.HIGHEST, preferred_element_type=jnp.float32
    )
    mean = stats[0:1] / members
    spread = stats[1:2] / members - mean * mean
    factor = lax.rsqrt(spread + eps_value)
    gains = gain[...]

    def scaled(span):
        value = value_ref[span, :].astype(jnp.float32)
        value = (value - mean) * factor * gains
        if active:
            value = jax.nn.silu(value)
        return value.astype(jnp.bfloat16)

    for step in range(tokens // (2 * block)):
        first = slice(step * block, (step + 1) * block)
        second = slice(tokens // 2 + step * block, tokens // 2 + (step + 1) * block)
        early, late = scaled(first), scaled(second)
        outs[0][first, :] = early[:, :main]
        outs[0][second, :] = late[:, :main]
        if len(outs) > 1:
            outs[1][first, :] = jnp.concatenate([early[:, main:], late[:, main:]], axis=1)


def normalized(value, near, far, gain, active, group_width, members):
    tokens, chunk = value.shape
    tail = chunk % 128 == 64 and chunk > 128
    vmem = pl.BlockSpec(memory_space=pltpu.VMEM)
    shapes = [jax.ShapeDtypeStruct((tokens, chunk - (64 if tail else 0)), jnp.bfloat16)]
    if tail:
        shapes = shapes + [jax.ShapeDtypeStruct((tokens // 2, 128), jnp.bfloat16)]
    return pl.pallas_call(
        functools.partial(norm_kernel, active, 64, group_width, members),
        out_shape=tuple(shapes),
        in_specs=[vmem] * 4,
        out_specs=tuple([vmem] * len(shapes)),
        compiler_params=pltpu.CompilerParams(vmem_limit_bytes=10 * 2**20),
    )(value, near, far, gain[None])


def gather_kernel(count, width, rim, kinds, *refs):
    owns, refs = refs[:kinds], refs[kinds:]
    full, refs = refs[0], refs[1:]
    slots, refs = refs[:kinds], refs[kinds:]
    if rim:
        edges, refs = refs[:kinds], refs[kinds:]
        send_sem, recv_sem, edge_send, edge_recv = refs
    else:
        send_sem, recv_sem = refs
    place = lax.axis_index("ch")
    row = lax.axis_index("row")
    steps = count.bit_length() - 1
    tokens = owns[0].shape[0]
    main = owns[0].shape[1]
    chunk = full.shape[1] // count
    partner = {"row": flipped(row, 1)}
    upper = 1 - row % 2

    barrier = pltpu.get_barrier_semaphore()
    for step in range(steps):
        pl.semaphore_signal(barrier, inc=1, device_id={"ch": flipped(place, 2**step)}, device_id_type=MESH)
    if rim:
        pl.semaphore_signal(barrier, inc=1, device_id=partner, device_id_type=MESH)
    pl.semaphore_wait(barrier, steps + (1 if rim else 0))

    orders = (list(range(steps)), list(range(steps))[::-1])

    def hops(relative, half, step):
        bit = 2 ** orders[half][step]
        target = relative ^ bit
        copies = []
        for kind in range(kinds):
            part = owns[kind].shape[0] // 2
            span = pl.ds(half * part, part)
            source = owns[kind].at[span] if relative == 0 else slots[kind].at[relative, span]
            copy = pltpu.make_async_remote_copy(
                src_ref=source,
                dst_ref=slots[kind].at[target, span],
                send_sem=send_sem.at[kind, target, half],
                recv_sem=recv_sem.at[kind, target, half],
                device_id={"ch": flipped(place, bit)},
                device_id_type=MESH,
            )
            copy.start()
            copies.append(copy)
        return copies

    def edge_hops(relative):
        copies = []
        for kind in range(kinds):
            begin = pl.multiple_of(upper * (owns[kind].shape[0] - width), width)
            span = pl.ds(begin, width)
            source = owns[kind].at[span] if relative == 0 else slots[kind].at[relative, span]
            copy = pltpu.make_async_remote_copy(
                src_ref=source,
                dst_ref=edges[kind].at[relative],
                send_sem=edge_send.at[kind, relative],
                recv_sem=edge_recv.at[kind, relative],
                device_id=partner,
                device_id_type=MESH,
            )
            copy.start()
            copies.append(copy)
        return copies

    def reached(half, step):
        found = [0]
        for earlier in range(step):
            found = found + [value ^ 2 ** orders[half][earlier] for value in found]
        return found

    sent = []
    edges_sent = []
    arrived = [set(), set()]
    done = {}

    def forward(relative, half, step):
        copies = hops(relative, half, step)
        done[(relative ^ 2 ** orders[half][step], half)] = copies
        sent.extend(copies)

    for step in range(steps):
        for half in (0, 1):
            forward(0, half, step)
    if rim:
        edges_sent.extend(edge_hops(0))

    top = width if rim else 0
    middle = tokens // 2

    def place_chunk(slot, parts):
        for index in range(count):

            @pl.when(slot == index)
            def _():
                base = index * chunk
                full[top : top + tokens, base : base + main] = parts[0]
                if kinds > 1:
                    full[top : top + middle, base + main : base + chunk] = parts[1][:, : chunk - main]
                    full[top + middle : top + tokens, base + main : base + chunk] = parts[1][:, chunk - main :]

    def absolute(relative):
        return combined(place, relative, steps)

    place_chunk(place, [ref[...] for ref in owns])

    for step in range(steps):
        for half in (0, 1):
            bit = 2 ** orders[half][step]
            for relative in [value ^ bit for value in reached(half, step)]:
                for copy in done[(relative, half)]:
                    copy.wait_recv()
                arrived[half].add(relative)
                for later in range(step + 1, steps):
                    forward(relative, half, later)
                if relative in arrived[1 - half]:
                    if rim:
                        edges_sent.extend(edge_hops(relative))
                    place_chunk(absolute(relative), [ref[relative] for ref in slots])
    for copy in sent:
        copy.wait_send()
    if rim:
        for copy in edges_sent:
            copy.wait()
        above_scale = (1 - upper).astype(jnp.float32)
        below_scale = upper.astype(jnp.float32)
        for index in range(count):
            slot = combined(place, index, steps)
            values = edges[0][slot].astype(jnp.float32)
            base = index * chunk
            full[0:width, base : base + main] = (values * above_scale).astype(full.dtype)
            full[top + tokens :, base : base + main] = (values * below_scale).astype(full.dtype)
            if kinds > 1:
                values = edges[1][slot].astype(jnp.float32)
                high_lanes, low_lanes = values[:, chunk - main :], values[:, : chunk - main]
                full[0:width, base + main : base + chunk] = (high_lanes * above_scale).astype(full.dtype)
                full[top + tokens :, base + main : base + chunk] = (low_lanes * below_scale).astype(full.dtype)


def gathered(parts, width, rim, number):
    count = lax.axis_size("ch")
    kinds = len(parts)
    tokens = parts[0].shape[0]
    chunk = sum(part.shape[0] * part.shape[1] for part in parts) // tokens
    high = tokens + (2 * width if rim else 0)
    vmem = pl.BlockSpec(memory_space=pltpu.VMEM)
    dma = pltpu.SemaphoreType.DMA
    scratch = [pltpu.VMEM((count, *part.shape), part.dtype) for part in parts]
    if rim:
        scratch = scratch + [pltpu.VMEM((count, width, part.shape[1]), part.dtype) for part in parts]
    scratch = scratch + [dma((kinds, count, 2)), dma((kinds, count, 2))]
    if rim:
        scratch = scratch + [dma((kinds, count)), dma((kinds, count))]
    return pl.pallas_call(
        functools.partial(gather_kernel, count, width, rim, kinds),
        out_shape=jax.ShapeDtypeStruct((high, count * chunk), parts[0].dtype),
        in_specs=[vmem] * kinds,
        out_specs=vmem,
        scratch_shapes=scratch,
        compiler_params=pltpu.CompilerParams(collective_id=number, has_side_effects=True, vmem_limit_bytes=14 * 2**20),
    )(*parts)


def conv_kernel(width, lanes, padded, weight, extra, out, stats, shifted):
    tap = pl.program_id(0)
    high, depth = padded.shape
    tokens = out.shape[0]

    @pl.when(tap == 0)
    def _():
        @pl.loop(0, depth // lanes)
        def _(block):
            span = pl.ds(pl.multiple_of(block * lanes, lanes), lanes)
            value = padded[:, span].astype(jnp.float32)
            column = lax.broadcasted_iota(jnp.int32, value.shape, 0) % width
            before = jnp.where(column == 0, 0.0, pltpu.roll(value, 1, 0))
            after = jnp.where(column == width - 1, 0.0, pltpu.roll(value, high - 1, 0))
            shifted[0, :, span] = before.astype(shifted.dtype)
            shifted[1, :, span] = padded[:, span]
            shifted[2, :, span] = after.astype(shifted.dtype)

    start = pl.multiple_of((tap // 3) * width, width)
    product = right_product(shifted[tap % 3, pl.ds(start, tokens), :], weight[0])

    @pl.when(tap == 0)
    def _():
        out[...] = product + extra[...].astype(jnp.float32)

    @pl.when(tap > 0)
    def _():
        out[...] += product

    @pl.when(tap == pl.num_programs(0) - 1)
    def _():
        value = out[...]
        stats[0:1] = jnp.sum(value, axis=0, keepdims=True)
        stats[1:2] = jnp.sum(value * value, axis=0, keepdims=True)


def conv_taps(padded, weight, extra, width):
    high, depth = padded.shape
    outs = weight.shape[0]
    taps = jnp.transpose(weight, (1, 2, 0, 3)).reshape(-1, outs, depth)
    tokens = high - 2 * width
    count = taps.shape[0]
    return pl.pallas_call(
        functools.partial(conv_kernel, width, 128),
        grid=(count,),
        out_shape=(
            jax.ShapeDtypeStruct((tokens, outs), jnp.float32),
            jax.ShapeDtypeStruct((2, outs), jnp.float32),
        ),
        in_specs=[
            pl.BlockSpec((high, depth), lambda tap: (0, 0)),
            pl.BlockSpec((1, outs, depth), lambda tap: (tap, 0, 0)),
            pl.BlockSpec(extra.shape, lambda tap: (0, 0)),
        ],
        out_specs=(
            pl.BlockSpec((tokens, outs), lambda tap: (0, 0)),
            pl.BlockSpec((2, outs), lambda tap: (0, 0)),
        ),
        scratch_shapes=[pltpu.VMEM((3, high, depth), padded.dtype)],
        compiler_params=pltpu.CompilerParams(vmem_limit_bytes=18 * 2**20),
        cost_estimate=pl.CostEstimate(
            flops=2 * count * tokens * outs * depth, bytes_accessed=count * outs * depth * 2, transcendentals=0
        ),
    )(padded, taps, extra)


def body(
    latent,
    timestep,
    norm_gain_a,
    conv_weight_a,
    time_weight,
    norm_gain_b,
    conv_weight_b,
    norm_gain_c,
    w_query,
    w_key,
    w_value,
    w_out,
):
    rows, width, local_ch = latent.shape
    span = H // rows
    place = lax.axis_index("row")
    image_id = place // span
    group_width = C // GROUPS
    members = float(H * width * group_width)
    tokens = rows * width

    def channel_sums(flat):
        return jnp.stack([jnp.sum(flat, axis=0), jnp.sum(flat * flat, axis=0)])

    def group_norm(flat, channel, gain, active):
        far = swapped(channel, "row", 0)
        return normalized(flat, channel, far, gain, active, group_width, members)

    def convolve(active, weight, extra, number):
        return conv_taps(gathered(active, width, True, number), weight, extra, width)

    image_ids = jnp.arange(timestep.shape[0])
    step_value = jnp.sum(jnp.where(image_ids == image_id, timestep, 0)).astype(jnp.float32)
    half = TDIM // 2
    freqs = jnp.exp(-math.log(10000.0) * jnp.arange(half, dtype=jnp.float32) / half)
    angles = step_value * freqs
    sinus = jnp.concatenate([jnp.cos(angles), jnp.sin(angles)])[None, :].astype(jnp.bfloat16)
    time_add = jax.nn.silu(jnp.dot(sinus, time_weight, preferred_element_type=jnp.float32))
    source = latent.reshape(tokens, local_ch)
    active_a = group_norm(source, channel_sums(source.astype(jnp.float32)), norm_gain_a, True)
    hidden_a, sums_a = convolve(active_a, conv_weight_a, time_add, 0)
    active_b = group_norm(hidden_a, sums_a, norm_gain_b, True)
    hidden_b, sums_b = convolve(active_b, conv_weight_b, source, 1)
    normed = group_norm(hidden_b, sums_b, norm_gain_c, False)
    inner = w_query.shape[0]
    projections = jnp.concatenate([w_query, w_key, w_value], axis=0)
    weight_cols = projections
    mixed = right_product(gathered(normed, width, False, 2), weight_cols)
    query = mixed[:, :inner].astype(jnp.bfloat16)
    keyed = mixed[:, inner : 2 * inner].astype(jnp.bfloat16)
    valued = mixed[:, 2 * inner :].astype(jnp.bfloat16)
    key_value = jnp.stack([keyed, valued])
    key_value = jnp.concatenate([key_value, swapped(key_value, "row", 0)], axis=1)
    local_heads = inner // HEAD_DIM
    query_heads = query.reshape(tokens, local_heads, HEAD_DIM)
    key_heads = key_value[0].reshape(-1, local_heads, HEAD_DIM)
    value_heads = key_value[1].reshape(-1, local_heads, HEAD_DIM)
    scores = jnp.einsum(
        "qhd,khd->hqk", query_heads, key_heads, preferred_element_type=jnp.float32
    ) * (1.0 / math.sqrt(HEAD_DIM))
    highest = jnp.max(scores, axis=-1, keepdims=True)
    raised = jnp.exp(scores - highest)
    weights = (raised / jnp.sum(raised, axis=-1, keepdims=True)).astype(jnp.bfloat16)
    heads_out = jnp.einsum("hqk,khd->qhd", weights, value_heads, preferred_element_type=jnp.float32)
    heads_out = heads_out.astype(jnp.bfloat16).reshape(tokens, inner)
    weight_cols = w_out
    projected = right_product(gathered((heads_out,), width, False, 3), weight_cols)
    total = hidden_b + projected
    return total.reshape(rows, width, local_ch).astype(jnp.bfloat16)


def solution(mesh):
    return jax.shard_map(
        body,
        mesh=mesh,
        in_specs=(
            P("row", None, "ch"),
            P(),
            P("ch"),
            P("ch", None, None, None),
            P(None, "ch"),
            P("ch"),
            P("ch", None, None, None),
            P("ch"),
            P("ch", None),
            P("ch", None),
            P("ch", None),
            P("ch", None),
        ),
        out_specs=P("row", None, "ch"),
        check_vma=False,
    )
```

time: 278 us -> 108 us (0.39)
  waiting for transfers between devices: 183 us -> 3.39 us
  Pallas kernels: 0 us -> 79.8 us
  local copies, waits for them, and re-layouts: 32 us -> 5.64 us
  matrix products: 30.8 us -> 13.5 us
  between operations: 14.3 us -> 0.94 us
  other arithmetic: 15.9 us -> 2.76 us
    all_gather x4 -> x0, waiting for transfers between devices: 179 us -> none  [the longest x2 124 us: convolve(): full = lax.all_gather(active, 'ch', axis=2, tiled=True)]
    pallas_call x0 -> x9, Pallas kernels: none -> 79.8 us  [the longest x4 58.2 us: gathered(): pl.pallas_call(functools.partial(gather_kernel, count, width, rim, kinds)...]
    conv_general_dilated x2 -> x0, matrix products: 15.6 us -> none  [conv_taps(): lax.conv_general_dilated(padded[None], weight, (1, 1), 'VALID', dimension...]
    all_gather x2 -> x0, local copies, waits for them, and re-layouts: 12 us -> none  [convolve(): full = lax.all_gather(active, 'ch', axis=2, tiled=True)]
    select_n x4 -> x0, other arithmetic: 9.8 us -> none  [the longest x2 6.06 us: facing_row(): return jnp.where(upper_half, field[-1:], field[:1])]
    convert_element_type x4 -> x0, local copies, waits for them, and re-layouts: 4.73 us -> none  [the longest x1 1.96 us: body(): jax.nn.silu(group_norm(hidden_a, norm_gain_b)).astype(jnp.bfloat16)]
    select_n x6 -> x0, local copies, waits for them, and re-layouts: 4.01 us -> none  [the longest x2 2.54 us: attach_rim(): above = jnp.where(upper_half, empty_row, partner)]
  transfers between devices with their start and end apart: 10 -> 4, of which waited for: 8 -> 3; matrix products, arithmetic and copies ran while one was open for 5% -> 3% of each run, Pallas kernels for 0% -> 0%
where the time goes in v1:
time: 108 us; the launch traced here: 107 us
  Pallas kernels  79.8 us (74%)
  matrix products  13.5 us (12%)
  local copies, waits for them, and re-layouts  5.64 us (5%)
  waiting for transfers between devices  3.39 us (3%)
  other arithmetic  2.76 us (3%)
  starting transfers between devices  1.45 us (1%)
    pallas_call x4, Pallas kernels, gathered(): pl.pallas_call(functools.partial(gather_kernel, count, width, rim, kinds)...  58.2 us
    pallas_call x2, Pallas kernels, conv_taps(): pl.pallas_call(functools.partial(conv_kernel, width, 128), grid=(count,),...  19.8 us
    dot_general x1, matrix products, body(): jnp.einsum('hqk,khd->qhd', weights, value_heads, preferred_element_type=j...  4.83 us
    sub x1, matrix products, body(): raised = jnp.exp(scores - highest)  4.82 us
    unnamed x20, local copies, waits for them, and re-layouts  4.12 us
    ppermute x4, waiting for transfers between devices, swapped(): return lax.ppermute(value, axis, pairs)  3.39 us
    dot_general x2, matrix products, right_product(): lax.dot_general(left, weight, (((1,), (1,)), ((), ())), preferred_element...  2.69 us
  transfers between devices with their start and end apart: 4, of which 3 were waited for; matrix products, arithmetic and copies ran while one was open for 3% of the time, Pallas kernels for 0%

profile of v1, /device:TPU:0, one launch (start us, length us, event | category | flops | bytes accessed | tf_op | source)
XLA Modules:
  0.0 107.4 jit_solution(10739853066278052124)
XLA Ops:
  0.0 1.2 %convert_reduce_fusion = (f32[320]{0:T(512)S(1)}, f32[320]{0:T(512)S(1)}) fusion(bf16[16,32,320]{2,1,0:T(8,128)(2,1)} %param.12), kind=kLoop, calls=%fused_computation.20 | loop fusion | flops 654720 | bytes 330240 | tf_op jit(solution)/shard_map/reduce_sum | solution.py:348
  1.2 0.6 collective-permute-start
  1.8 1.3 %fusion.20 = s32[]{:T(128)} fusion(s32[4]{0:T(128)} %param.13, s32[]{:T(128)S(6)} %select_n.9), kind=kLoop, calls=%fused_computation.33 | loop fusion | flops 11 | bytes 24 | tf_op jit(solution)/shard_map/reduce_sum | solution.py:358
  3.9 1.1 %convolution_reduce_fusion = f32[320]{0:T(512)S(1)} fusion(bf16[320,1]{0,1:T(2,128)(2,1)S(1)} %reshape.38, bf16[320,320]{1,0:T(8,128)(2,1)} %param.16), kind=kOutput, calls=%fused_computation.17 | convolution fusion | flops 204800 | bytes 206720 | tf_op jit(solution)/shard_map/dot_general | solution.py:363
  5.0 0.7 broadcast_in_dim.16.refs_3_
  5.7 1.0 copy-done.1
  6.7 0.6 shard_map.118
  7.4 17.2 %shard_map.119.padded = bf16[576,1280]{1,0:T(8,128)(2,1)S(1)} custom-call(bf16[512,256]{1,0:T(8,128)(2,1)S(1)} %get-tuple-element.15.refs_0_, bf16[256,128]{1,0:T(8,128)(2,1)S(1)} %get-tuple-element.16.refs_1_), custom_call_target="tpu_custom_call" | custom-call | tf_op jit(solution)/shard_map/pallas_call | solution.py:249
  24.6 3.1 %copy-done.3 = bf16[320,3,3,1280]{3,0,2,1:T(8,128)(2,1)S(1)} copy-done((bf16[320,3,3,1280]{3,0,2,1:T(8,128)(2,1)S(1)}, bf16[320,3,3,1280]{3,0,2,1:T(8,128)(2,1)}, u32[]{:S(2)}) %copy-start.3) | copy-done | bytes 7372824
  27.7 9.9 %shard_map.120 = (f32[512,320]{1,0:T(8,128)S(1)}, f32[2,320]{1,0:T(2,128)S(1)}) custom-call(bf16[576,1280]{1,0:T(8,128)(2,1)S(1)} %shard_map.119.padded, bf16[9,320,1280]{2,1,0:T(8,128)(2,1)S(1)} %bitcast.30, f32[1,320]{1,0:T(1,128)S(1)} %mul.28.extra), custom_call_target="tpu_custom_call" | custom-call | flops 3774873600 | bytes 7372800 | tf_op jit(solution)/shard_map/pallas_call | solution.py:301
  38.1 0.8 collective-permute-done.1.refs_2_
  38.9 0.6 shard_map.121
  39.5 15.1 %shard_map.122.padded = bf16[576,1280]{1,0:T(8,128)(2,1)S(1)} custom-call(bf16[512,256]{1,0:T(8,128)(2,1)S(1)} %get-tuple-element.19.refs_0_, bf16[256,128]{1,0:T(8,128)(2,1)S(1)} %get-tuple-element.20.refs_1_), custom_call_target="tpu_custom_call" | custom-call | tf_op jit(solution)/shard_map/pallas_call | solution.py:249
  54.7 9.8 %shard_map.123 = (f32[512,320]{1,0:T(8,128)S(1)}, f32[2,320]{1,0:T(2,128)S(1)}) custom-call(bf16[576,1280]{1,0:T(8,128)(2,1)S(1)} %shard_map.122.padded, bf16[9,320,1280]{2,1,0:T(8,128)(2,1)S(1)} %bitcast.31, bf16[512,320]{1,0:T(8,128)(2,1)S(1)} %bitcast.29), custom_call_target="tpu_custom_call" | custom-call | flops 3774873600 | bytes 7372800 | tf_op jit(solution)/shard_map/pallas_call | solution.py:301
  64.6 0.4 collective-permute-start.2
  65.0 0.8 collective-permute-done.2.refs_2_
  65.8 0.6 shard_map.124
  66.4 14.4 %shard_map.125 = bf16[512,1280]{1,0:T(8,128)(2,1)S(1)} custom-call(bf16[512,256]{1,0:T(8,128)(2,1)S(1)} %get-tuple-element.23.refs_0_, bf16[256,128]{1,0:T(8,128)(2,1)S(1)} %get-tuple-element.24.refs_1_), custom_call_target="tpu_custom_call" | custom-call | tf_op jit(solution)/shard_map/pallas_call | solution.py:249
  80.8 1.2 %fusion.12 = bf16[512,768]{1,0:T(8,128)(2,1)S(1)} fusion(bf16[512,1280]{1,0:T(8,128)(2,1)S(1)} %shard_map.125, bf16[256,1280]{1,0:T(8,128)(2,1)S(1)} %copy-done.7, bf16[256,1280]{1,0:T(8,128)(2,1)S(1)} %copy-done.8, bf16[256,1280]{1,0:T(8,128)(2,1)S(1)} %copy-done.9), kind=kOutput, calls=%fused_computation.13 | convolution fusion | flops 1012924416 | bytes 4063232 | tf_op jit(solution)/shard_map/dot_general | solution.py:29
  82.4 1.7 %collective-permute-done.3 = bf16[2,512,256]{2,1,0:T(8,128)(2,1)S(1)} collective-permute-done((bf16[2,512,256]{2,1,0:T(8,128)(2,1)S(1)}, bf16[2,512,256]{2,1,0:T(8,128)(2,1)S(1)}, u32[]{:S(2)}, u32[]{:S(2)}) %collective-permute-start.3) | collective-permute-done | bytes 524320 | tf_op jit(solution)/shard_map/ppermute | solution.py:25
  84.7 4.8 %fusion.25 = (f32[4,512]{1,0:T(4,128)S(1)}, f32[4,512,1024]{2,1,0:T(8,128)}) fusion(bf16[512,4,64]{0,2,1:T(8,128)(2,1)S(1)} %bitcast.34, bf16[1024,4,64]{0,2,1:T(8,128)(2,1)S(1)} %bitcast.32), kind=kOutput, calls=%fused_computation.38 | convolution fusion | flops 274727936 | bytes 9183232 | tf_op jit(solution)/shard_map/sub | solution.py:387
  89.5 4.8 %fusion.16 = bf16[4,64,512]{2,1,0:T(8,128)(2,1)S(1)} fusion(bf16[1024,4,64]{0,2,1:T(8,128)(2,1)S(1)} %bitcast.33, f32[4,512,1024]{2,1,0:T(8,128)} %get-tuple-element.33, f32[4,512]{1,0:T(4,128)S(1)} %get-tuple-element.32), kind=kOutput, calls=%fused_computation.16 | convolution fusion | flops 272760832 | bytes 9183232 | tf_op jit(solution)/shard_map/hqk,khd->qhd/dot_general | solution.py:389
  94.5 11.5 %shard_map.126 = bf16[512,1024]{1,0:T(8,128)(2,1)S(1)} custom-call(bf16[512,256]{1,0:T(8,128)(2,1)S(1)} %copy.21.refs_0_), custom_call_target="tpu_custom_call" | custom-call | tf_op jit(solution)/shard_map/pallas_call | solution.py:249
  106.0 1.5 %fusion.15 = bf16[512,320]{1,0:T(8,128)(2,1)} fusion(f32[512,320]{1,0:T(8,128)S(1)} %get-tuple-element.21.refs_0_, bf16[512,1024]{1,0:T(8,128)(2,1)S(1)} %shard_map.126, bf16[320,1024]{1,0:T(8,128)(2,1)S(1)} %copy-done), kind=kOutput, calls=%fused_computation.15 | convolution fusion | flops 335872000 | bytes 2686976 | tf_op jit(solution)/shard_map/dot_general | solution.py:29
  (39 shorter events, 1.6 us)
Async XLA Ops:
  0.0 106.0 %copy-start = (bf16[320,1024]{1,0:T(8,128)(2,1)S(1)}, bf16[320,1024]{1,0:T(8,128)(2,1)}, u32[]{:S(2)}) copy-start(bf16[320,1024]{1,0:T(8,128)(2,1)} %param.23) | copy-start | bytes 1966084
  1.2 4.5 %collective-permute-start = (f32[2,320]{1,0:T(2,128)S(1)}, f32[2,320]{1,0:T(2,128)S(1)}, u32[]{:S(2)}, u32[]{:S(2)}) collective-permute-start(f32[2,320]{1,0:T(2,128)S(1)} %pad_maximum_fusion.2.refs_1_), channel_id=1, source_target_pairs={{0,1},{1,0},{2,3},{3,2},{4,5},{5,4},{6,7},{7,6},{8,9},{9,8},{10,11... | collective-permute-start | bytes 7688 | tf_op jit(solution)/shard_map/ppermute | solution.py:25
  5.7 1.0 copy-start.1
  24.6 3.1 %copy-start.3 = (bf16[320,3,3,1280]{3,0,2,1:T(8,128)(2,1)S(1)}, bf16[320,3,3,1280]{3,0,2,1:T(8,128)(2,1)}, u32[]{:S(2)}) copy-start(bf16[320,3,3,1280]{3,0,2,1:T(8,128)(2,1)} %param.15) | copy-start | bytes 22118404
  27.7 10.3 %copy-start.5 = (f32[320]{0:T(512)S(1)}, f32[320]{0:T(512)}, u32[]{:S(2)}) copy-start(f32[320]{0:T(512)} %param.17) | copy-start | bytes 3844
  27.7 26.9 %copy-start.2 = (bf16[16,32,320]{2,1,0:T(8,128)(2,1)S(1)}, bf16[16,32,320]{2,1,0:T(8,128)(2,1)}, u32[]{:S(2)}) copy-start(bf16[16,32,320]{2,1,0:T(8,128)(2,1)} %param.12) | copy-start | bytes 983044
  27.7 26.9 %copy-start.4 = (bf16[320,3,3,1280]{3,0,2,1:T(8,128)(2,1)S(1)}, bf16[320,3,3,1280]{3,0,2,1:T(8,128)(2,1)}, u32[]{:S(2)}) copy-start(bf16[320,3,3,1280]{3,0,2,1:T(8,128)(2,1)} %param.18) | copy-start | bytes 22118404
  37.6 1.2 %collective-permute-start.1 = (f32[2,320]{1,0:T(2,128)S(1)}, f32[2,320]{1,0:T(2,128)S(1)}, u32[]{:S(2)}, u32[]{:S(2)}) collective-permute-start(f32[2,320]{1,0:T(2,128)S(1)} %get-tuple-element.18.refs_1_), channel_id=1, source_target_pairs={{0,1},{1,0},{2,3},{3,2},{4,5},{5,4},{6,7},{7,6},{8,9},{9,8},{10,11... | collective-permute-start | bytes 7688 | tf_op jit(solution)/shard_map/ppermute | solution.py:25
  54.6 10.3 %copy-start.6 = (f32[320]{0:T(512)S(1)}, f32[320]{0:T(512)}, u32[]{:S(2)}) copy-start(f32[320]{0:T(512)} %param.19) | copy-start | bytes 3844
  54.7 26.1 %copy-start.7 = (bf16[256,1280]{1,0:T(8,128)(2,1)S(1)}, bf16[256,1280]{1,0:T(8,128)(2,1)}, u32[]{:S(2)}) copy-start(bf16[256,1280]{1,0:T(8,128)(2,1)} %param.22) | copy-start | bytes 1966084
  54.7 26.1 %copy-start.8 = (bf16[256,1280]{1,0:T(8,128)(2,1)S(1)}, bf16[256,1280]{1,0:T(8,128)(2,1)}, u32[]{:S(2)}) copy-start(bf16[256,1280]{1,0:T(8,128)(2,1)} %param.21) | copy-start | bytes 1966084
  54.7 26.1 %copy-start.9 = (bf16[256,1280]{1,0:T(8,128)(2,1)S(1)}, bf16[256,1280]{1,0:T(8,128)(2,1)}, u32[]{:S(2)}) copy-start(bf16[256,1280]{1,0:T(8,128)(2,1)} %param.20) | copy-start | bytes 1966084
  64.6 1.2 %collective-permute-start.2 = (f32[2,320]{1,0:T(2,128)S(1)}, f32[2,320]{1,0:T(2,128)S(1)}, u32[]{:S(2)}, u32[]{:S(2)}) collective-permute-start(f32[2,320]{1,0:T(2,128)S(1)} %get-tuple-element.22.refs_1_), channel_id=1, source_target_pairs={{0,1},{1,0},{2,3},{3,2},{4,5},{5,4},{6,7},{7,6},{8,9},{9,8},{10,11... | collective-permute-start | bytes 7688 | tf_op jit(solution)/shard_map/ppermute | solution.py:25
  82.1 2.0 %collective-permute-start.3 = (bf16[2,512,256]{2,1,0:T(8,128)(2,1)S(1)}, bf16[2,512,256]{2,1,0:T(8,128)(2,1)S(1)}, u32[]{:S(2)}, u32[]{:S(2)}) collective-permute-start(bf16[2,512,256]{2,1,0:T(8,128)(2,1)S(1)} %pad_maximum_fusion.1), channel_id=1, source_target_pairs={{0,1},{1,0},{2,3},{3,2},{4,5},{5,4},{6,7},{7,6},{8,9},{9,8},{10,11... | collective-permute-start | bytes 1572872 | tf_op jit(solution)/shard_map/ppermute | solution.py:25

commit v2 on v1

--- a/solution.py
+++ b/solution.py
@@ -274,8 +274,10 @@
             shifted[1, :, span] = padded[:, span]
             shifted[2, :, span] = after.astype(shifted.dtype)
 
-    start = pl.multiple_of((tap // 3) * width, width)
-    product = right_product(shifted[tap % 3, pl.ds(start, tokens), :], weight[0])
+    start = pl.multiple_of(tap * width, width)
+    product = right_product(shifted[0, pl.ds(start, tokens), :], weight[0])
+    for column in range(1, weight.shape[0]):
+        product = product + right_product(shifted[column, pl.ds(start, tokens), :], weight[column])
 
     @pl.when(tap == 0)
     def _():
@@ -300,14 +302,14 @@
     count = taps.shape[0]
     return pl.pallas_call(
         functools.partial(conv_kernel, width, 128),
-        grid=(count,),
+        grid=(count // 3,),
         out_shape=(
             jax.ShapeDtypeStruct((tokens, outs), jnp.float32),
             jax.ShapeDtypeStruct((2, outs), jnp.float32),
         ),
         in_specs=[
             pl.BlockSpec((high, depth), lambda tap: (0, 0)),
-            pl.BlockSpec((1, outs, depth), lambda tap: (tap, 0, 0)),
+            pl.BlockSpec((3, outs, depth), lambda tap: (tap, 0, 0)),
             pl.BlockSpec(extra.shape, lambda tap: (0, 0)),
         ],
         out_specs=(
@@ -315,7 +317,7 @@
             pl.BlockSpec((2, outs), lambda tap: (0, 0)),
         ),
         scratch_shapes=[pltpu.VMEM((3, high, depth), padded.dtype)],
-        compiler_params=pltpu.CompilerParams(vmem_limit_bytes=18 * 2**20),
+        compiler_params=pltpu.CompilerParams(vmem_limit_bytes=22 * 2**20),
         cost_estimate=pl.CostEstimate(
             flops=2 * count * tokens * outs * depth, bytes_accessed=count * outs * depth * 2, transcendentals=0
         ),

time: 108 us -> 104 us (0.963)
  Pallas kernels: 79.8 us -> 76.3 us
    pallas_call x2, Pallas kernels: 19.8 us -> 16.3 us  [conv_taps(): pl.pallas_call(functools.partial(conv_kernel, width, 128), grid=(count //...]
where the time goes in v2:
time: 104 us
  Pallas kernels  76.3 us (73%)
  matrix products  13.5 us (13%)
  local copies, waits for them, and re-layouts  5.64 us (5%)
  waiting for transfers between devices  3.39 us (3%)
  other arithmetic  2.76 us (3%)
  starting transfers between devices  1.45 us (1%)
    pallas_call x4, Pallas kernels, gathered(): pl.pallas_call(functools.partial(gather_kernel, count, width, rim, kinds)...  58.2 us
    pallas_call x2, Pallas kernels, conv_taps(): pl.pallas_call(functools.partial(conv_kernel, width, 128), grid=(count //...  16.3 us
    dot_general x1, matrix products, body(): jnp.einsum('hqk,khd->qhd', weights, value_heads, preferred_element_type=j...  4.83 us
    sub x1, matrix products, body(): raised = jnp.exp(scores - highest)  4.82 us
    unnamed x20, local copies, waits for them, and re-layouts  4.12 us
    ppermute x4, waiting for transfers between devices, swapped(): return lax.ppermute(value, axis, pairs)  3.39 us
    dot_general x2, matrix products, right_product(): lax.dot_general(left, weight, (((1,), (1,)), ((), ())), preferred_element...  2.69 us
  transfers between devices with their start and end apart: 4, of which 3 were waited for; matrix products, arithmetic and copies ran while one was open for 3% of the time, Pallas kernels for 0%

profile of v2, /device:TPU:0, one launch (start us, length us, event | category | flops | bytes accessed | tf_op | source)
XLA Modules:
  0.0 104.0 jit_solution(9815107838962163609)
XLA Ops:
  0.0 1.2 %convert_reduce_fusion = (f32[320]{0:T(512)S(1)}, f32[320]{0:T(512)S(1)}) fusion(bf16[16,32,320]{2,1,0:T(8,128)(2,1)} %param.12), kind=kLoop, calls=%fused_computation.20 | loop fusion | flops 654720 | bytes 330240 | tf_op jit(solution)/shard_map/reduce_sum | solution.py:350
  1.2 0.6 collective-permute-start
  1.8 1.3 %fusion.20 = s32[]{:T(128)} fusion(s32[4]{0:T(128)} %param.13, s32[]{:T(128)S(6)} %select_n.9), kind=kLoop, calls=%fused_computation.33 | loop fusion | flops 11 | bytes 24 | tf_op jit(solution)/shard_map/reduce_sum | solution.py:360
  3.9 1.1 %convolution_reduce_fusion = f32[320]{0:T(512)S(1)} fusion(bf16[320,1]{0,1:T(2,128)(2,1)S(1)} %reshape.38, bf16[320,320]{1,0:T(8,128)(2,1)} %param.16), kind=kOutput, calls=%fused_computation.17 | convolution fusion | flops 204800 | bytes 206720 | tf_op jit(solution)/shard_map/dot_general | solution.py:365
  5.0 0.7 broadcast_in_dim.16.refs_3_
  5.7 1.0 copy-done.1
  6.7 0.6 shard_map.118
  7.4 17.2 %shard_map.119.padded = bf16[576,1280]{1,0:T(8,128)(2,1)S(1)} custom-call(bf16[512,256]{1,0:T(8,128)(2,1)S(1)} %get-tuple-element.15.refs_0_, bf16[256,128]{1,0:T(8,128)(2,1)S(1)} %get-tuple-element.16.refs_1_), custom_call_target="tpu_custom_call" | custom-call | tf_op jit(solution)/shard_map/pallas_call | solution.py:249
  24.6 3.1 %copy-done.3 = bf16[320,3,3,1280]{3,0,2,1:T(8,128)(2,1)S(1)} copy-done((bf16[320,3,3,1280]{3,0,2,1:T(8,128)(2,1)S(1)}, bf16[320,3,3,1280]{3,0,2,1:T(8,128)(2,1)}, u32[]{:S(2)}) %copy-start.3) | copy-done | bytes 7372824
  27.7 8.1 %shard_map.120 = (f32[512,320]{1,0:T(8,128)S(1)}, f32[2,320]{1,0:T(2,128)S(1)}) custom-call(bf16[576,1280]{1,0:T(8,128)(2,1)S(1)} %shard_map.119.padded, bf16[9,320,1280]{2,1,0:T(8,128)(2,1)S(1)} %bitcast.30, f32[1,320]{1,0:T(1,128)S(1)} %mul.28.extra), custom_call_target="tpu_custom_call" | custom-call | flops 3774873600 | bytes 7372800 | tf_op jit(solution)/shard_map/pallas_call | solution.py:303
  36.3 0.8 collective-permute-done.1.refs_2_
  37.1 0.6 shard_map.121
  37.7 15.1 %shard_map.122.padded = bf16[576,1280]{1,0:T(8,128)(2,1)S(1)} custom-call(bf16[512,256]{1,0:T(8,128)(2,1)S(1)} %get-tuple-element.19.refs_0_, bf16[256,128]{1,0:T(8,128)(2,1)S(1)} %get-tuple-element.20.refs_1_), custom_call_target="tpu_custom_call" | custom-call | tf_op jit(solution)/shard_map/pallas_call | solution.py:249
  52.9 8.1 %shard_map.123 = (f32[512,320]{1,0:T(8,128)S(1)}, f32[2,320]{1,0:T(2,128)S(1)}) custom-call(bf16[576,1280]{1,0:T(8,128)(2,1)S(1)} %shard_map.122.padded, bf16[9,320,1280]{2,1,0:T(8,128)(2,1)S(1)} %bitcast.31, bf16[512,320]{1,0:T(8,128)(2,1)S(1)} %bitcast.29), custom_call_target="tpu_custom_call" | custom-call | flops 3774873600 | bytes 7372800 | tf_op jit(solution)/shard_map/pallas_call | solution.py:303
  61.1 0.4 collective-permute-start.2
  61.5 0.8 collective-permute-done.2.refs_2_
  62.3 0.6 shard_map.124
  62.9 14.4 %shard_map.125 = bf16[512,1280]{1,0:T(8,128)(2,1)S(1)} custom-call(bf16[512,256]{1,0:T(8,128)(2,1)S(1)} %get-tuple-element.23.refs_0_, bf16[256,128]{1,0:T(8,128)(2,1)S(1)} %get-tuple-element.24.refs_1_), custom_call_target="tpu_custom_call" | custom-call | tf_op jit(solution)/shard_map/pallas_call | solution.py:249
  77.3 1.2 %fusion.12 = bf16[512,768]{1,0:T(8,128)(2,1)S(1)} fusion(bf16[512,1280]{1,0:T(8,128)(2,1)S(1)} %shard_map.125, bf16[256,1280]{1,0:T(8,128)(2,1)S(1)} %copy-done.7, bf16[256,1280]{1,0:T(8,128)(2,1)S(1)} %copy-done.8, bf16[256,1280]{1,0:T(8,128)(2,1)S(1)} %copy-done.9), kind=kOutput, calls=%fused_computation.13 | convolution fusion | flops 1012924416 | bytes 4063232 | tf_op jit(solution)/shard_map/dot_general | solution.py:29
  78.9 1.7 %collective-permute-done.3 = bf16[2,512,256]{2,1,0:T(8,128)(2,1)S(1)} collective-permute-done((bf16[2,512,256]{2,1,0:T(8,128)(2,1)S(1)}, bf16[2,512,256]{2,1,0:T(8,128)(2,1)S(1)}, u32[]{:S(2)}, u32[]{:S(2)}) %collective-permute-start.3) | collective-permute-done | bytes 524320 | tf_op jit(solution)/shard_map/ppermute | solution.py:25
  81.2 4.8 %fusion.25 = (f32[4,512]{1,0:T(4,128)S(1)}, f32[4,512,1024]{2,1,0:T(8,128)}) fusion(bf16[512,4,64]{0,2,1:T(8,128)(2,1)S(1)} %bitcast.34, bf16[1024,4,64]{0,2,1:T(8,128)(2,1)S(1)} %bitcast.32), kind=kOutput, calls=%fused_computation.38 | convolution fusion | flops 274727936 | bytes 9183232 | tf_op jit(solution)/shard_map/sub | solution.py:389
  86.0 4.8 %fusion.16 = bf16[4,64,512]{2,1,0:T(8,128)(2,1)S(1)} fusion(bf16[1024,4,64]{0,2,1:T(8,128)(2,1)S(1)} %bitcast.33, f32[4,512,1024]{2,1,0:T(8,128)} %get-tuple-element.33, f32[4,512]{1,0:T(4,128)S(1)} %get-tuple-element.32), kind=kOutput, calls=%fused_computation.16 | convolution fusion | flops 272760832 | bytes 9183232 | tf_op jit(solution)/shard_map/hqk,khd->qhd/dot_general | solution.py:391
  91.0 11.5 %shard_map.126 = bf16[512,1024]{1,0:T(8,128)(2,1)S(1)} custom-call(bf16[512,256]{1,0:T(8,128)(2,1)S(1)} %copy.21.refs_0_), custom_call_target="tpu_custom_call" | custom-call | tf_op jit(solution)/shard_map/pallas_call | solution.py:249
  102.5 1.5 %fusion.15 = bf16[512,320]{1,0:T(8,128)(2,1)} fusion(f32[512,320]{1,0:T(8,128)S(1)} %get-tuple-element.21.refs_0_, bf16[512,1024]{1,0:T(8,128)(2,1)S(1)} %shard_map.126, bf16[320,1024]{1,0:T(8,128)(2,1)S(1)} %copy-done), kind=kOutput, calls=%fused_computation.15 | convolution fusion | flops 335872000 | bytes 2686976 | tf_op jit(solution)/shard_map/dot_general | solution.py:29
  (39 shorter events, 1.6 us)
Async XLA Ops:
  0.0 102.5 %copy-start = (bf16[320,1024]{1,0:T(8,128)(2,1)S(1)}, bf16[320,1024]{1,0:T(8,128)(2,1)}, u32[]{:S(2)}) copy-start(bf16[320,1024]{1,0:T(8,128)(2,1)} %param.23) | copy-start | bytes 1966084
  1.2 4.5 %collective-permute-start = (f32[2,320]{1,0:T(2,128)S(1)}, f32[2,320]{1,0:T(2,128)S(1)}, u32[]{:S(2)}, u32[]{:S(2)}) collective-permute-start(f32[2,320]{1,0:T(2,128)S(1)} %pad_maximum_fusion.2.refs_1_), channel_id=1, source_target_pairs={{0,1},{1,0},{2,3},{3,2},{4,5},{5,4},{6,7},{7,6},{8,9},{9,8},{10,11... | collective-permute-start | bytes 7688 | tf_op jit(solution)/shard_map/ppermute | solution.py:25
  5.7 1.0 copy-start.1
  24.6 3.1 %copy-start.3 = (bf16[320,3,3,1280]{3,0,2,1:T(8,128)(2,1)S(1)}, bf16[320,3,3,1280]{3,0,2,1:T(8,128)(2,1)}, u32[]{:S(2)}) copy-start(bf16[320,3,3,1280]{3,0,2,1:T(8,128)(2,1)} %param.15) | copy-start | bytes 22118404
  27.7 8.6 %copy-start.5 = (f32[320]{0:T(512)S(1)}, f32[320]{0:T(512)}, u32[]{:S(2)}) copy-start(f32[320]{0:T(512)} %param.17) | copy-start | bytes 3844
  27.7 25.1 %copy-start.2 = (bf16[16,32,320]{2,1,0:T(8,128)(2,1)S(1)}, bf16[16,32,320]{2,1,0:T(8,128)(2,1)}, u32[]{:S(2)}) copy-start(bf16[16,32,320]{2,1,0:T(8,128)(2,1)} %param.12) | copy-start | bytes 983044
  27.7 25.2 %copy-start.4 = (bf16[320,3,3,1280]{3,0,2,1:T(8,128)(2,1)S(1)}, bf16[320,3,3,1280]{3,0,2,1:T(8,128)(2,1)}, u32[]{:S(2)}) copy-start(bf16[320,3,3,1280]{3,0,2,1:T(8,128)(2,1)} %param.18) | copy-start | bytes 22118404
  35.9 1.2 %collective-permute-start.1 = (f32[2,320]{1,0:T(2,128)S(1)}, f32[2,320]{1,0:T(2,128)S(1)}, u32[]{:S(2)}, u32[]{:S(2)}) collective-permute-start(f32[2,320]{1,0:T(2,128)S(1)} %get-tuple-element.18.refs_1_), channel_id=1, source_target_pairs={{0,1},{1,0},{2,3},{3,2},{4,5},{5,4},{6,7},{7,6},{8,9},{9,8},{10,11... | collective-permute-start | bytes 7688 | tf_op jit(solution)/shard_map/ppermute | solution.py:25
  52.9 8.6 %copy-start.6 = (f32[320]{0:T(512)S(1)}, f32[320]{0:T(512)}, u32[]{:S(2)}) copy-start(f32[320]{0:T(512)} %param.19) | copy-start | bytes 3844
  52.9 24.4 %copy-start.7 = (bf16[256,1280]{1,0:T(8,128)(2,1)S(1)}, bf16[256,1280]{1,0:T(8,128)(2,1)}, u32[]{:S(2)}) copy-start(bf16[256,1280]{1,0:T(8,128)(2,1)} %param.22) | copy-start | bytes 1966084
  52.9 24.4 %copy-start.8 = (bf16[256,1280]{1,0:T(8,128)(2,1)S(1)}, bf16[256,1280]{1,0:T(8,128)(2,1)}, u32[]{:S(2)}) copy-start(bf16[256,1280]{1,0:T(8,128)(2,1)} %param.21) | copy-start | bytes 1966084
  52.9 24.4 %copy-start.9 = (bf16[256,1280]{1,0:T(8,128)(2,1)S(1)}, bf16[256,1280]{1,0:T(8,128)(2,1)}, u32[]{:S(2)}) copy-start(bf16[256,1280]{1,0:T(8,128)(2,1)} %param.20) | copy-start | bytes 1966084
  61.1 1.2 %collective-permute-start.2 = (f32[2,320]{1,0:T(2,128)S(1)}, f32[2,320]{1,0:T(2,128)S(1)}, u32[]{:S(2)}, u32[]{:S(2)}) collective-permute-start(f32[2,320]{1,0:T(2,128)S(1)} %get-tuple-element.22.refs_1_), channel_id=1, source_target_pairs={{0,1},{1,0},{2,3},{3,2},{4,5},{5,4},{6,7},{7,6},{8,9},{9,8},{10,11... | collective-permute-start | bytes 7688 | tf_op jit(solution)/shard_map/ppermute | solution.py:25
  78.6 2.0 %collective-permute-start.3 = (bf16[2,512,256]{2,1,0:T(8,128)(2,1)S(1)}, bf16[2,512,256]{2,1,0:T(8,128)(2,1)S(1)}, u32[]{:S(2)}, u32[]{:S(2)}) collective-permute-start(bf16[2,512,256]{2,1,0:T(8,128)(2,1)S(1)} %pad_maximum_fusion.1), channel_id=1, source_target_pairs={{0,1},{1,0},{2,3},{3,2},{4,5},{5,4},{6,7},{7,6},{8,9},{9,8},{10,11... | collective-permute-start | bytes 1572872 | tf_op jit(solution)/shard_map/ppermute | solution.py:25
